TPU v7x, 32 devices: a whole 2x2x4 slice. The times are simulated.
32 devices in a mesh: seq: 4 (over y, core), exp: 8 (over z, x).
Axes of the slice: x: 2, y: 2, z: 4, core: 2. Of those that a mesh axis runs over, the one named last changes fastest.
Arguments:
- queries: bfloat16 [2048, 4096], P('seq', 'exp'), may hold values from -6 to 6
- key_rows: bfloat16 [2048, 512], P('seq', 'exp'), may hold values from -6 to 6
- value_rows: bfloat16 [2048, 512], P('seq', 'exp'), may hold values from -6 to 6
- sink_logits: float32 [64], P('exp'), may hold values from 0 to 6
- out_proj: bfloat16 [4096, 2560], P('exp'), may hold values from -0.09375 to 0.09375
- residual: bfloat16 [2048, 2560], P(('seq', 'exp')), may hold values from -0.59765625 to 0.59765625
- norm_gain: float32 [2560], replicated, may hold values from 0.25 to 1.75
- expert_ids: int32 [2048, 4], P(('seq', 'exp')), may hold values from 0 to 31, all different within a row; in each aligned block of 64 rows (0 to 63, 64 to 127, ...) at most 16 rows name the same one
- gate_weights: float32 [2048, 4], P(('seq', 'exp')), may hold values from 0.2 to 1
- w_gate_up: bfloat16 [32, 2560, 2880], P(('seq', 'exp')), may hold values from -0.125 to 0.125
- w_down: bfloat16 [32, 1440, 2560], P(('seq', 'exp')), may hold values from -0.15625 to 0.15625
Outputs:
- layer_out: bfloat16 [2048, 2560], P(('seq', 'exp'))
Inputs may be any that keep to these rules, and one draw needn't show every extreme that they name: `expert_ids`: each row names 4 different experts. In the rows of one device (aligned blocks of 64 rows) no expert is named more than 16 times, and in every draw some expert is named exactly 16 times in some block.
All inputs are finite; a program needn't handle non-finite values.
Results may differ from a plain program's by a relative error of at most 0.022.
Values may be sent and summed in bfloat16 or wider, within the bound.
No kernel may reach another device: no remote copies, remote signals or barrier semaphores. Data moves between devices by JAX's collectives and lax.ppermute only.
A program may use at most 128 MiB of HBM per device.

v0:
```python
import math

import jax
import jax.numpy as jnp
from jax import lax
from jax.sharding import Mesh
from jax.sharding import PartitionSpec as P

KVH = 8
WINDOW = 128
SEQ = ("y", "c")
EXP = ("z", "x")


def factors(mesh):
    seq, exp = mesh.shape["seq"], mesh.shape["exp"]
    nc = 2 if seq % 2 == 0 else 1
    nz = 1
    while nz * nz < exp:
        nz *= 2
    return seq // nc, nc, nz, exp // nz


def swapped(value, axis, apart):
    return lax.ppermute(value, axis, [(i, i ^ 1 << apart) for i in range(lax.axis_size(axis))])


def shifted(block, axis, distance):
    devices = range(lax.axis_size(axis))
    route = [(i - distance, i) for i in devices if i - distance in devices]
    return lax.ppermute(block, axis, route)


def rotated(value, axis, by):
    size = lax.axis_size(axis)
    return lax.ppermute(value, axis, [(i, (i + by) % size) for i in range(size)])


def in_plane(value, dy, dx):
    ny, nx = lax.axis_size("y"), lax.axis_size("x")
    route = [
        (y * nx + x, (y + dy) % ny * nx + (x + dx) % nx) for y in range(ny) for x in range(nx)
    ]
    return lax.ppermute(value, ("y", "x"), route)


def window_attention(
    query_rows, key_block, value_block, prior_keys, prior_values, sink_row, first_index, window_size
):
    row_count = query_rows.shape[0]
    head_width_dim = key_block.shape[1]
    head_count = query_rows.shape[1] // head_width_dim
    block_count = row_count // window_size
    key_ext = jnp.concatenate([prior_keys, key_block], axis=0)
    value_ext = jnp.concatenate([prior_values, value_block], axis=0)
    key_block_tiles = jnp.concatenate(
        [
            key_ext[:row_count].reshape(block_count, window_size, head_width_dim),
            key_block.reshape(block_count, window_size, head_width_dim),
        ],
        axis=1,
    )
    value_block_tiles = jnp.concatenate(
        [
            value_ext[:row_count].reshape(block_count, window_size, head_width_dim),
            value_block.reshape(block_count, window_size, head_width_dim),
        ],
        axis=1,
    )
    query_block_tiles = query_rows.reshape(block_count, window_size, head_count, head_width_dim)
    attention_scores = jnp.einsum(
        "xnem,xcm->xenc", query_block_tiles, key_block_tiles, preferred_element_type=jnp.float32
    ) * (1.0 / math.sqrt(head_width_dim))
    query_pos = jnp.arange(window_size, dtype=jnp.int32)[:, None]
    key_pos = jnp.arange(2 * window_size, dtype=jnp.int32)[None, :]
    inside = (key_pos > query_pos) & (key_pos <= query_pos + window_size)
    block_start = first_index + jnp.arange(block_count, dtype=jnp.int32) * window_size
    present = block_start[:, None] - window_size + key_pos >= 0
    allowed = inside[None, None, :, :] & present[:, None, None, :]
    attention_scores = jnp.where(allowed, attention_scores, -jnp.inf)
    sink_grid = sink_row[None, :, None, None]
    highest = jnp.maximum(jnp.max(attention_scores, axis=-1, keepdims=True), sink_grid)
    raised = jnp.exp(attention_scores - highest)
    totals = jnp.sum(raised, axis=-1, keepdims=True) + jnp.exp(sink_grid - highest)
    attention_probabilities = (raised / totals).astype(jnp.bfloat16)
    mixed_value_rows = jnp.einsum(
        "emjt,eta->ejma",
        attention_probabilities,
        value_block_tiles,
        preferred_element_type=jnp.float32,
    )
    return mixed_value_rows.astype(jnp.bfloat16).reshape(row_count, head_count * head_width_dim)


def expert_rows(rows_in, gate_up, down_rows):
    hidden_units = gate_up.shape[1] // 2
    both = jnp.dot(rows_in, gate_up, preferred_element_type=jnp.float32)
    gate_part = both[:, :hidden_units]
    up_part = both[:, hidden_units:]
    activated = (gate_part * jax.nn.sigmoid(1.702 * gate_part) * (up_part + 1.0)).astype(
        jnp.bfloat16
    )
    return jnp.dot(activated, down_rows, preferred_element_type=jnp.float32).astype(jnp.bfloat16)


def per_device(
    queries,
    key_rows,
    value_rows,
    sink_logits,
    out_proj,
    residual,
    norm_gain,
    expert_ids,
    gate_weights,
    w_gate_up,
    w_down,
):
    f32, bf16 = jnp.float32, jnp.bfloat16
    ny, nc, nz, nx = (lax.axis_size(a) for a in ("y", "c", "z", "x"))
    yi, ci, zi, xi = (lax.axis_index(a) for a in ("y", "c", "z", "x"))
    seq_index = yi * nc + ci
    exp_index = zi * nx + xi
    local_rows = queries.shape[0]
    width = out_proj.shape[1]
    tokens = local_rows // (nz * nx)
    expert_total = ny * nc * nz * nx
    top_count = expert_ids.shape[1]
    cap = 2 * top_count * tokens // expert_total

    group_devices = nz * nx // KVH
    key_piece = key_rows
    value_piece = value_rows
    for bit_number in range(group_devices.bit_length() - 1):
        other_keys, other_values = swapped((key_piece, value_piece), EXP, bit_number)
        upper_half = jnp.right_shift(exp_index, bit_number) & 1 == 1
        key_piece = jnp.where(
            upper_half,
            jnp.concatenate([other_keys, key_piece], axis=1),
            jnp.concatenate([key_piece, other_keys], axis=1),
        )
        value_piece = jnp.where(
            upper_half,
            jnp.concatenate([other_values, value_piece], axis=1),
            jnp.concatenate([value_piece, other_values], axis=1),
        )
    prior_keys, prior_values = shifted(
        (key_piece[local_rows - WINDOW :], value_piece[local_rows - WINDOW :]), SEQ, 1
    )

    flat_ids = expert_ids.reshape(-1)
    chosen = (flat_ids[:, None] == jnp.arange(expert_total, dtype=jnp.int32)[None, :]).astype(
        jnp.int32
    )
    slot_rank = jnp.sum((jnp.cumsum(chosen, axis=0) - chosen) * chosen, axis=1)
    slot_index = (flat_ids * cap + slot_rank).reshape(tokens, top_count)
    facts = jnp.concatenate([slot_index.astype(f32), gate_weights], axis=1)
    facts_of = [facts] + [rotated(facts, "z", k) for k in range(1, nz)]

    places = jnp.arange(ny * nx * nc * cap, dtype=jnp.int32)
    rank, rest = places % cap, places // cap
    to_c, rest = (ci + rest % nc) % nc, rest // nc
    to_x, to_y = (xi + rest % nx) % nx, (yi + rest // nx) % ny
    plane_slots = (((to_y * nc + to_c) * nz + zi) * nx + to_x) * cap + rank
    plane_rows = ny * nx * nc * cap

    attended = window_attention(
        queries,
        key_piece,
        value_piece,
        prior_keys,
        prior_values,
        sink_logits,
        seq_index * local_rows,
        WINDOW,
    )
    partial = jnp.dot(attended, out_proj, preferred_element_type=f32).astype(bf16)

    def rows_of(z, x):
        return lax.dynamic_slice(partial, ((z % nz * nx + x % nx) * tokens, 0), (tokens, width))

    crossed = []
    for step in range(nz):
        block = zi - 1 - step + 2 * nz
        crossed.append(
            [rotated(rows_of(block, xi + dx), "x", dx) for dx in range(1, nx)]
            + [rows_of(block, xi)]
        )
    running = None
    for step in range(nz):
        total = sum(piece.astype(f32) for piece in crossed[step])
        if running is not None:
            total = total + rotated(running, "z", 1).astype(f32)
        running = total.astype(bf16)
    hidden = residual.astype(f32) + total
    scale = lax.rsqrt(jnp.mean(hidden * hidden, axis=-1, keepdims=True) + 1e-05)
    normed = (hidden * scale * norm_gain[None, :]).astype(bf16)

    offsets = [(dy, dx) for dy in range(ny) for dx in range(nx)]
    arriving = normed
    landed = []
    spreads = []
    for k in range(nz):
        if k:
            arriving = rotated(arriving, "z", 1)
        slots = facts_of[k][:, :top_count].astype(jnp.int32)
        hits = plane_slots[None, None, :] == slots[:, :, None]
        spread = jnp.sum(jnp.where(hits, facts_of[k][:, top_count:, None], 0.0), axis=1)
        spreads.append(spread)
        placing = jnp.any(hits, axis=1).astype(bf16)
        placed = lax.dot_general(
            placing, arriving, (((0,), (0,)), ((), ())), preferred_element_type=f32
        ).astype(bf16)
        placed = placed.reshape(ny * nx, nc, cap, width)
        landed.append(
            jnp.stack([placed[0]] + [in_plane(placed[j], *offsets[j]) for j in range(1, ny * nx)])
        )

    groups = [list(range(min(2, nz)))] + [[k] for k in range(2, nz)]
    returned = [None] * nz
    for group in groups:
        mine = jnp.stack([landed[k][:, 0] for k in group])
        given = [mine]
        for dc in range(1, nc):
            given.append(rotated(jnp.stack([landed[k][:, dc] for k in group]), "c", dc))
        rows_in = jnp.stack(given)
        results = expert_rows(rows_in.reshape(-1, width), w_gate_up[0], w_down[0])
        results = results.reshape(rows_in.shape)
        back = [results[0]]
        for dc in range(1, nc):
            back.append(rotated(results[dc], "c", -dc))
        for i, k in enumerate(group):
            returned[k] = jnp.stack([part[i] for part in back], axis=1)

    running = None
    for k in list(range(1, nz)) + [0]:
        rows_back = jnp.stack(
            [returned[k][0]]
            + [in_plane(returned[k][j], -offsets[j][0], -offsets[j][1]) for j in range(1, ny * nx)]
        ).reshape(plane_rows, width)
        high = spreads[k].astype(bf16)
        low = (spreads[k] - high.astype(f32)).astype(bf16)
        total = jnp.dot(high, rows_back, preferred_element_type=f32) + jnp.dot(
            low, rows_back, preferred_element_type=f32
        )
        if running is not None:
            total = total + rotated(running, "z", 1).astype(f32)
        running = total.astype(bf16)
    return (hidden + total).astype(bf16)


def solution(mesh):
    sizes = factors(mesh)
    inner = Mesh(mesh.devices.reshape(sizes), ("y", "c", "z", "x"))
    every = SEQ + EXP

    return jax.shard_map(
        per_device,
        mesh=inner,
        in_specs=(
            P(SEQ, EXP),
            P(SEQ, EXP),
            P(SEQ, EXP),
            P(EXP),
            P(EXP, None),
            P(every, None),
            P(),
            P(every, None),
            P(every, None),
            P(every, None, None),
            P(every, None, None),
        ),
        out_specs=P(every, None),
        check_vma=False,
    )
```

profile of v0, /device:TPU:0, one launch (start us, length us, event | category | flops | bytes accessed | tf_op | source)
XLA Modules:
  0.0 185.4 jit_solution(12046063926223923842)
XLA Ops:
  0.9 2.4 %collective-permute-start.1 = (bf16[128,64]{0,1:T(8,128)(2,1)S(1)}, bf16[128,64]{0,1:T(8,128)(2,1)S(1)}, u32[]{:S(2)}, u32[]{:S(2)}) collective-permute-start(bf16[128,64]{0,1:T(8,128)(2,1)S(1)} %slice.238), channel_id=1, source_target_pairs={{0,8},{8,16},{16,24},{1,9},{9,17},{17,25},{2,10},{10,18},{18,26},{... | collective-permute-start | bytes 49160 | tf_op jit(solution)/shard_map/ppermute | solution.py:31
  4.0 4.5 %collective-permute-start = (bf16[128,64]{0,1:T(8,128)(2,1)S(1)}, bf16[128,64]{0,1:T(8,128)(2,1)S(1)}, u32[]{:S(2)}, u32[]{:S(2)}) collective-permute-start(bf16[128,64]{0,1:T(8,128)(2,1)S(1)} %slice.236), channel_id=1, source_target_pairs={{0,8},{8,16},{16,24},{1,9},{9,17},{17,25},{2,10},{10,18},{18,26},{... | collective-permute-start | bytes 49160 | tf_op jit(solution)/shard_map/ppermute | solution.py:31
  10.7 2.4 %reshape.344 = bf16[4,128,8,64]{3,2,1,0:T(8,128)(2,1)} reshape(bf16[512,512]{1,0:T(8,128)(2,1)} %param.11) | data formatting | bytes 1048576 | tf_op jit(solution)/shard_map/reshape | solution.py:70
  19.7 3.0 %convolution_convert_fusion = bf16[512,2560]{1,0:T(8,128)(2,1)} fusion(bf16[512,2560]{1,0:T(8,128)(2,1)S(1)} %copy-done, bf16[64,8,4,128]{3,2,1,0:T(4,128)(2,1)S(1)} %bitcast.262), kind=kOutput, calls=%fused_computation.12 | convolution fusion | flops 1343488000 | bytes 5767168 | tf_op jit(solution)/shard_map/dot_general | solution.py:177
  29.5 6.4 %collective-permute-done.5 = bf16[64,2560]{1,0:T(8,128)(2,1)} collective-permute-done((bf16[64,2560]{1,0:T(8,128)(2,1)}, bf16[64,2560]{1,0:T(8,128)(2,1)}, u32[]{:S(2)}, u32[]{:S(2)}) %collective-permute-start.5) | collective-permute-done | bytes 327712 | tf_op jit(solution)/shard_map/ppermute | solution.py:36
  40.1 2.7 %collective-permute-start.33 = (f32[64,8]{0,1:T(8,128)S(1)}, f32[64,8]{0,1:T(8,128)S(1)}, u32[]{:S(2)}, u32[]{:S(2)}) collective-permute-start(f32[64,8]{0,1:T(8,128)S(1)} %pad_maximum_fusion.18), channel_id=1, source_target_pairs={{0,4},{2,6},{4,0},{6,2},{1,5},{3,7},{5,1},{7,3},{8,12},{10,14},{12... | collective-permute-start | bytes 6152 | tf_op jit(solution)/shard_map/ppermute | solution.py:36
  51.0 3.6 %collective-permute-done.3 = bf16[64,2560]{1,0:T(8,128)(2,1)S(1)} collective-permute-done((bf16[64,2560]{1,0:T(8,128)(2,1)S(1)}, bf16[64,2560]{1,0:T(8,128)(2,1)S(1)}, u32[]{:S(2)}, u32[]{:S(2)}) %collective-permute-start.3) | collective-permute-done | bytes 327712 | tf_op jit(solution)/shard_map/ppermute | solution.py:36
  54.5 3.7 %collective-permute-done.7 = bf16[64,2560]{1,0:T(8,128)(2,1)S(1)} collective-permute-done((bf16[64,2560]{1,0:T(8,128)(2,1)S(1)}, bf16[64,2560]{1,0:T(8,128)(2,1)S(1)}, u32[]{:S(2)}, u32[]{:S(2)}) %collective-permute-start.7) | collective-permute-done | bytes 327712 | tf_op jit(solution)/shard_map/ppermute | solution.py:36
  59.7 8.6 %collective-permute-done.8 = bf16[64,2560]{1,0:T(8,128)(2,1)S(1)} collective-permute-done((bf16[64,2560]{1,0:T(8,128)(2,1)S(1)}, bf16[64,2560]{1,0:T(8,128)(2,1)S(1)}, u32[]{:S(2)}, u32[]{:S(2)}) %collective-permute-start.8) | collective-permute-done | bytes 327712 | tf_op jit(solution)/shard_map/ppermute | solution.py:36
  70.5 2.6 %collective-permute-start.11 = (bf16[2,16,2560]{2,1,0:T(8,128)(2,1)S(1)}, bf16[2,16,2560]{2,1,0:T(8,128)(2,1)S(1)}, u32[]{:S(2)}, u32[]{:S(2)}) collective-permute-start(bf16[2,16,2560]{2,1,0:T(8,128)(2,1)S(1)} %bitcast.294), channel_id=1, source_target_pairs={{0,17},{1,16},{16,1},{17,0},{2,19},{3,18},{18,3},{19,2},{4,21},{5,... | collective-permute-start | bytes 491528 | tf_op jit(solution)/shard_map/ppermute | solution.py:44
  74.1 3.2 %collective-permute-done.10 = bf16[2,16,2560]{2,1,0:T(8,128)(2,1)S(1)} collective-permute-done((bf16[2,16,2560]{2,1,0:T(8,128)(2,1)S(1)}, bf16[2,16,2560]{2,1,0:T(8,128)(2,1)S(1)}, u32[]{:S(2)}, u32[]{:S(2)}) %collective-permute-start.10) | collective-permute-done | bytes 163872 | tf_op jit(solution)/shard_map/ppermute | solution.py:44
  78.8 4.1 %collective-permute-done.13 = bf16[64,2560]{1,0:T(8,128)(2,1)S(1)} collective-permute-done((bf16[64,2560]{1,0:T(8,128)(2,1)S(1)}, bf16[64,2560]{1,0:T(8,128)(2,1)S(1)}, u32[]{:S(2)}, u32[]{:S(2)}) %collective-permute-start.13) | collective-permute-done | bytes 327712 | tf_op jit(solution)/shard_map/ppermute | solution.py:36
  88.8 3.2 %collective-permute-done.15 = bf16[2,16,2560]{2,1,0:T(8,128)(2,1)S(1)} collective-permute-done((bf16[2,16,2560]{2,1,0:T(8,128)(2,1)S(1)}, bf16[2,16,2560]{2,1,0:T(8,128)(2,1)S(1)}, u32[]{:S(2)}, u32[]{:S(2)}) %collective-permute-start.15) | collective-permute-done | bytes 163872 | tf_op jit(solution)/shard_map/ppermute | solution.py:44
  92.3 3.6 %collective-permute-done.23 = bf16[64,2560]{1,0:T(8,128)(2,1)S(1)} collective-permute-done((bf16[64,2560]{1,0:T(8,128)(2,1)S(1)}, bf16[64,2560]{1,0:T(8,128)(2,1)S(1)}, u32[]{:S(2)}, u32[]{:S(2)}) %collective-permute-start.23) | collective-permute-done | bytes 327712 | tf_op jit(solution)/shard_map/ppermute | solution.py:36
  101.8 3.2 %collective-permute-done.35 = bf16[2,16,2560]{2,1,0:T(8,128)(2,1)S(1)} collective-permute-done((bf16[2,16,2560]{2,1,0:T(8,128)(2,1)S(1)}, bf16[2,16,2560]{2,1,0:T(8,128)(2,1)S(1)}, u32[]{:S(2)}, u32[]{:S(2)}) %collective-permute-start.35) | collective-permute-done | bytes 163872 | tf_op jit(solution)/shard_map/ppermute | solution.py:44
  105.2 3.9 %collective-permute-done.24 = bf16[64,2560]{1,0:T(8,128)(2,1)S(1)} collective-permute-done((bf16[64,2560]{1,0:T(8,128)(2,1)S(1)}, bf16[64,2560]{1,0:T(8,128)(2,1)S(1)}, u32[]{:S(2)}, u32[]{:S(2)}) %collective-permute-start.24) | collective-permute-done | bytes 327712 | tf_op jit(solution)/shard_map/ppermute | solution.py:36
  113.2 4.1 %fusion = f32[128,2880]{0,1:T(8,128)S(1)} fusion(bf16[128,2560]{1,0:T(8,128)(2,1)S(1)} %bitcast.260, bf16[1,2560,2880]{1,2,0:T(8,128)(2,1)S(1)} %bitcast.251), kind=kOutput, calls=%fused_computation | convolution fusion | flops 1887436800 | bytes 16875520 | tf_op jit(solution)/shard_map/dot_general | solution.py:97
  119.8 5.6 %fusion.4 = f32[256,2880]{0,1:T(8,128)} fusion(bf16[256,2560]{1,0:T(8,128)(2,1)S(1)} %bitcast.267, bf16[1,2560,2880]{1,2,0:T(8,128)(2,1)S(1)} %bitcast.251), kind=kOutput, calls=%fused_computation.4 | convolution fusion | flops 3774873600 | bytes 19005440 | tf_op jit(solution)/shard_map/dot_general | solution.py:97
  125.4 4.2 %fusion.12 = bf16[256,2560]{1,0:T(8,128)(2,1)S(1)} fusion(bf16[1,1440,2560]{2,1,0:T(8,128)(2,1)S(1)} %bitcast.317, f32[256,2880]{0,1:T(8,128)} %fusion.4), kind=kOutput, calls=%fused_computation.16 | convolution fusion | flops 1891041280 | bytes 11632640 | tf_op jit(solution)/shard_map/dot_general | solution.py:103
  133.5 4.3 %fusion.2 = f32[128,2880]{0,1:T(8,128)S(1)} fusion(bf16[128,2560]{1,0:T(8,128)(2,1)S(1)} %bitcast.261, bf16[1,2560,2880]{1,2,0:T(8,128)(2,1)S(1)} %bitcast.251), kind=kOutput, calls=%fused_computation.2 | convolution fusion | flops 1887436800 | bytes 16875520 | tf_op jit(solution)/shard_map/dot_general | solution.py:97
  150.0 2.5 %collective-permute-done.43 = bf16[2,16,2560]{2,1,0:T(8,128)(2,1)S(1)} collective-permute-done((bf16[2,16,2560]{2,1,0:T(8,128)(2,1)S(1)}, bf16[2,16,2560]{2,1,0:T(8,128)(2,1)S(1)}, u32[]{:S(2)}, u32[]{:S(2)}) %collective-permute-start.43) | collective-permute-done | bytes 163872 | tf_op jit(solution)/shard_map/ppermute | solution.py:44
  154.7 7.3 %collective-permute-done.45 = bf16[64,2560]{1,0:T(8,128)(2,1)S(1)} collective-permute-done((bf16[64,2560]{1,0:T(8,128)(2,1)S(1)}, bf16[64,2560]{1,0:T(8,128)(2,1)S(1)}, u32[]{:S(2)}, u32[]{:S(2)}) %collective-permute-start.45) | collective-permute-done | bytes 327712 | tf_op jit(solution)/shard_map/ppermute | solution.py:36
  165.5 9.7 %collective-permute-done.46 = bf16[64,2560]{1,0:T(8,128)(2,1)S(1)} collective-permute-done((bf16[64,2560]{1,0:T(8,128)(2,1)S(1)}, bf16[64,2560]{1,0:T(8,128)(2,1)S(1)}, u32[]{:S(2)}, u32[]{:S(2)}) %collective-permute-start.46) | collective-permute-done | bytes 327712 | tf_op jit(solution)/shard_map/ppermute | solution.py:36
  175.9 8.5 %collective-permute-done.47 = bf16[64,2560]{1,0:T(8,128)(2,1)S(1)} collective-permute-done((bf16[64,2560]{1,0:T(8,128)(2,1)S(1)}, bf16[64,2560]{1,0:T(8,128)(2,1)S(1)}, u32[]{:S(2)}, u32[]{:S(2)}) %collective-permute-start.47) | collective-permute-done | bytes 327712 | tf_op jit(solution)/shard_map/ppermute | solution.py:36
  (193 shorter events, 77.2 us)
Async XLA Ops:
  0.9 13.1 %collective-permute-start.1 = (bf16[128,64]{0,1:T(8,128)(2,1)S(1)}, bf16[128,64]{0,1:T(8,128)(2,1)S(1)}, u32[]{:S(2)}, u32[]{:S(2)}) collective-permute-start(bf16[128,64]{0,1:T(8,128)(2,1)S(1)} %slice.238), channel_id=1, source_target_pairs={{0,8},{8,16},{16,24},{1,9},{9,17},{17,25},{2,10},{10,18},{18,26},{... | collective-permute-start | bytes 49160 | tf_op jit(solution)/shard_map/ppermute | solution.py:31
  4.0 14.1 %collective-permute-start = (bf16[128,64]{0,1:T(8,128)(2,1)S(1)}, bf16[128,64]{0,1:T(8,128)(2,1)S(1)}, u32[]{:S(2)}, u32[]{:S(2)}) collective-permute-start(bf16[128,64]{0,1:T(8,128)(2,1)S(1)} %slice.236), channel_id=1, source_target_pairs={{0,8},{8,16},{16,24},{1,9},{9,17},{17,25},{2,10},{10,18},{18,26},{... | collective-permute-start | bytes 49160 | tf_op jit(solution)/shard_map/ppermute | solution.py:31
  25.0 10.9 %collective-permute-start.5 = (bf16[64,2560]{1,0:T(8,128)(2,1)}, bf16[64,2560]{1,0:T(8,128)(2,1)}, u32[]{:S(2)}, u32[]{:S(2)}) collective-permute-start(bf16[64,2560]{1,0:T(8,128)(2,1)} %get-tuple-element.18), channel_id=1, source_target_pairs={{0,1},{1,0},{2,3},{3,2},{4,5},{5,4},{6,7},{7,6},{8,9},{9,8},{10,11... | collective-permute-start | bytes 983048 | tf_op jit(solution)/shard_map/ppermute | solution.py:36
  29.0 15.8 %collective-permute-start.4 = (bf16[64,2560]{1,0:T(8,128)(2,1)S(1)}, bf16[64,2560]{1,0:T(8,128)(2,1)}, u32[]{:S(2)}, u32[]{:S(2)}) collective-permute-start(bf16[64,2560]{1,0:T(8,128)(2,1)S(1)} %get-tuple-element.19), channel_id=1, source_target_pairs={{0,1},{1,0},{2,3},{3,2},{4,5},{5,4},{6,7},{7,6},{8,9},{9,8},{10,11... | collective-permute-start | bytes 983048 | tf_op jit(solution)/shard_map/ppermute | solution.py:36
  37.8 10.2 %collective-permute-start.6 = (bf16[64,2560]{1,0:T(8,128)(2,1)}, bf16[64,2560]{1,0:T(8,128)(2,1)}, u32[]{:S(2)}, u32[]{:S(2)}) collective-permute-start(bf16[64,2560]{1,0:T(8,128)(2,1)} %add_convert_fusion.2), channel_id=1, source_target_pairs={{0,2},{2,4},{4,6},{6,0},{1,3},{3,5},{5,7},{7,1},{8,10},{10,12},{12... | collective-permute-start | bytes 983048 | tf_op jit(solution)/shard_map/ppermute | solution.py:36
  44.1 15.3 %collective-permute-start.12 = (f32[64,8]{0,1:T(8,128)S(1)}, f32[64,8]{0,1:T(8,128)S(1)}, u32[]{:S(2)}, u32[]{:S(2)}) collective-permute-start(f32[64,8]{0,1:T(8,128)S(1)} %pad_maximum_fusion.18), channel_id=1, source_target_pairs={{0,2},{2,4},{4,6},{6,0},{1,3},{3,5},{5,7},{7,1},{8,10},{10,12},{12... | collective-permute-start | bytes 6152 | tf_op jit(solution)/shard_map/ppermute | solution.py:36
  44.8 9.8 %collective-permute-start.3 = (bf16[64,2560]{1,0:T(8,128)(2,1)S(1)}, bf16[64,2560]{1,0:T(8,128)(2,1)S(1)}, u32[]{:S(2)}, u32[]{:S(2)}) collective-permute-start(bf16[64,2560]{1,0:T(8,128)(2,1)S(1)} %get-tuple-element.20), channel_id=1, source_target_pairs={{0,1},{1,0},{2,3},{3,2},{4,5},{5,4},{6,7},{7,6},{8,9},{9,8},{10,11... | collective-permute-start | bytes 983048 | tf_op jit(solution)/shard_map/ppermute | solution.py:36
  49.4 10.2 %collective-permute-start.2 = (bf16[64,2560]{1,0:T(8,128)(2,1)S(1)}, bf16[64,2560]{1,0:T(8,128)(2,1)S(1)}, u32[]{:S(2)}, u32[]{:S(2)}) collective-permute-start(bf16[64,2560]{1,0:T(8,128)(2,1)S(1)} %get-tuple-element.17), channel_id=1, source_target_pairs={{0,1},{1,0},{2,3},{3,2},{4,5},{5,4},{6,7},{7,6},{8,9},{9,8},{10,11... | collective-permute-start | bytes 983048 | tf_op jit(solution)/shard_map/ppermute | solution.py:36
  92.2 27.4 %collective-permute-start.17 = (bf16[2,4,16,2560]{3,2,1,0:T(8,128)(2,1)S(1)}, bf16[2,4,16,2560]{3,2,1,0:T(8,128)(2,1)S(1)}, u32[]{:S(2)}, u32[]{:S(2)}) collective-permute-start(bf16[2,4,16,2560]{3,2,1,0:T(8,128)(2,1)S(1)} %pad_maximum_fusion.3), channel_id=1, source_target_pairs={{0,8},{8,0},{1,9},{9,1},{2,10},{10,2},{3,11},{11,3},{4,12},{12,4},... | collective-permute-start | bytes 1966088 | tf_op jit(solution)/shard_map/ppermute | solution.py:36
  109.6 9.4 %collective-permute-start.25 = (bf16[2,16,2560]{2,1,0:T(8,128)(2,1)S(1)}, bf16[2,16,2560]{2,1,0:T(8,128)(2,1)S(1)}, u32[]{:S(2)}, u32[]{:S(2)}) collective-permute-start(bf16[2,16,2560]{2,1,0:T(8,128)(2,1)S(1)} %bitcast.301), channel_id=1, source_target_pairs={{0,1},{1,0},{16,17},{17,16},{2,3},{3,2},{18,19},{19,18},{4,5},{5,4... | collective-permute-start | bytes 491528 | tf_op jit(solution)/shard_map/ppermute | solution.py:44
  118.8 11.0 %collective-permute-start.38 = (bf16[1,4,16,2560]{3,2,1,0:T(8,128)(2,1)S(1)}, bf16[1,4,16,2560]{3,2,1,0:T(8,128)(2,1)S(1)}, u32[]{:S(2)}, u32[]{:S(2)}) collective-permute-start(bf16[1,4,16,2560]{3,2,1,0:T(8,128)(2,1)S(1)} %bitcast.276), channel_id=1, source_target_pairs={{0,8},{8,0},{1,9},{9,1},{2,10},{10,2},{3,11},{11,3},{4,12},{12,4},... | collective-permute-start | bytes 983048 | tf_op jit(solution)/shard_map/ppermute | solution.py:36
  119.1 14.3 %collective-permute-start.28 = (bf16[1,4,16,2560]{3,2,1,0:T(8,128)(2,1)S(1)}, bf16[1,4,16,2560]{3,2,1,0:T(8,128)(2,1)S(1)}, u32[]{:S(2)}, u32[]{:S(2)}) collective-permute-start(bf16[1,4,16,2560]{3,2,1,0:T(8,128)(2,1)S(1)} %get-tuple-element.48), channel_id=1, source_target_pairs={{0,8},{8,0},{1,9},{9,1},{2,10},{10,2},{3,11},{11,3},{4,12},{12,4},... | collective-permute-start | bytes 983048 | tf_op jit(solution)/shard_map/ppermute | solution.py:36
  129.7 11.9 %collective-permute-start.18 = (bf16[2,4,16,2560]{3,2,1,0:T(8,128)(2,1)S(1)}, bf16[2,4,16,2560]{3,2,1,0:T(8,128)(2,1)S(1)}, u32[]{:S(2)}, u32[]{:S(2)}) collective-permute-start(bf16[2,4,16,2560]{3,2,1,0:T(8,128)(2,1)S(1)} %bitcast.273), channel_id=1, source_target_pairs={{0,8},{8,0},{1,9},{9,1},{2,10},{10,2},{3,11},{11,3},{4,12},{12,4},... | collective-permute-start | bytes 1966088 | tf_op jit(solution)/shard_map/ppermute | solution.py:36
  129.9 9.5 %collective-permute-start.39 = (bf16[2,16,2560]{2,1,0:T(8,128)(2,1)S(1)}, bf16[2,16,2560]{2,1,0:T(8,128)(2,1)S(1)}, u32[]{:S(2)}, u32[]{:S(2)}) collective-permute-start(bf16[2,16,2560]{2,1,0:T(8,128)(2,1)S(1)} %get-tuple-element.30), channel_id=1, source_target_pairs={{0,1},{1,0},{16,17},{17,16},{2,3},{3,2},{18,19},{19,18},{4,5},{5,4... | collective-permute-start | bytes 491528 | tf_op jit(solution)/shard_map/ppermute | solution.py:44
  131.4 9.8 %collective-permute-start.40 = (bf16[2,16,2560]{2,1,0:T(8,128)(2,1)S(1)}, bf16[2,16,2560]{2,1,0:T(8,128)(2,1)S(1)}, u32[]{:S(2)}, u32[]{:S(2)}) collective-permute-start(bf16[2,16,2560]{2,1,0:T(8,128)(2,1)S(1)} %get-tuple-element.32), channel_id=1, source_target_pairs={{0,16},{1,17},{16,0},{17,1},{2,18},{3,19},{18,2},{19,3},{4,20},{5,... | collective-permute-start | bytes 491528 | tf_op jit(solution)/shard_map/ppermute | solution.py:44
  131.7 9.5 %collective-permute-start.41 = (bf16[2,16,2560]{2,1,0:T(8,128)(2,1)S(1)}, bf16[2,16,2560]{2,1,0:T(8,128)(2,1)S(1)}, u32[]{:S(2)}, u32[]{:S(2)}) collective-permute-start(bf16[2,16,2560]{2,1,0:T(8,128)(2,1)S(1)} %get-tuple-element.31), channel_id=1, source_target_pairs={{0,17},{1,16},{16,1},{17,0},{2,19},{3,18},{18,3},{19,2},{4,21},{5,... | collective-permute-start | bytes 491528 | tf_op jit(solution)/shard_map/ppermute | solution.py:44
  142.3 10.2 %collective-permute-start.43 = (bf16[2,16,2560]{2,1,0:T(8,128)(2,1)S(1)}, bf16[2,16,2560]{2,1,0:T(8,128)(2,1)S(1)}, u32[]{:S(2)}, u32[]{:S(2)}) collective-permute-start(bf16[2,16,2560]{2,1,0:T(8,128)(2,1)S(1)} %get-tuple-element.26), channel_id=1, source_target_pairs={{0,16},{1,17},{16,0},{17,1},{2,18},{3,19},{18,2},{19,3},{4,20},{5,... | collective-permute-start | bytes 491528 | tf_op jit(solution)/shard_map/ppermute | solution.py:44
  145.3 18.2 %collective-permute-start.30 = (bf16[2,16,2560]{2,1,0:T(8,128)(2,1)S(1)}, bf16[2,16,2560]{2,1,0:T(8,128)(2,1)S(1)}, u32[]{:S(2)}, u32[]{:S(2)}) collective-permute-start(bf16[2,16,2560]{2,1,0:T(8,128)(2,1)S(1)} %get-tuple-element.42), channel_id=1, source_target_pairs={{0,1},{1,0},{16,17},{17,16},{2,3},{3,2},{18,19},{19,18},{4,5},{5,4... | collective-permute-start | bytes 491528 | tf_op jit(solution)/shard_map/ppermute | solution.py:44
  145.9 19.3 %collective-permute-start.31 = (bf16[2,16,2560]{2,1,0:T(8,128)(2,1)S(1)}, bf16[2,16,2560]{2,1,0:T(8,128)(2,1)S(1)}, u32[]{:S(2)}, u32[]{:S(2)}) collective-permute-start(bf16[2,16,2560]{2,1,0:T(8,128)(2,1)S(1)} %get-tuple-element.44), channel_id=1, source_target_pairs={{0,16},{1,17},{16,0},{17,1},{2,18},{3,19},{18,2},{19,3},{4,20},{5,... | collective-permute-start | bytes 491528 | tf_op jit(solution)/shard_map/ppermute | solution.py:44
  148.8 16.4 %collective-permute-start.32 = (bf16[2,16,2560]{2,1,0:T(8,128)(2,1)S(1)}, bf16[2,16,2560]{2,1,0:T(8,128)(2,1)S(1)}, u32[]{:S(2)}, u32[]{:S(2)}) collective-permute-start(bf16[2,16,2560]{2,1,0:T(8,128)(2,1)S(1)} %get-tuple-element.43), channel_id=1, source_target_pairs={{0,17},{1,16},{16,1},{17,0},{2,19},{3,18},{18,3},{19,2},{4,21},{5,... | collective-permute-start | bytes 491528 | tf_op jit(solution)/shard_map/ppermute | solution.py:44
  153.2 22.4 %collective-permute-start.19 = (bf16[2,16,2560]{2,1,0:T(8,128)(2,1)S(1)}, bf16[2,16,2560]{2,1,0:T(8,128)(2,1)S(1)}, u32[]{:S(2)}, u32[]{:S(2)}) collective-permute-start(bf16[2,16,2560]{2,1,0:T(8,128)(2,1)S(1)} %get-tuple-element.54), channel_id=1, source_target_pairs={{0,1},{1,0},{16,17},{17,16},{2,3},{3,2},{18,19},{19,18},{4,5},{5,4... | collective-permute-start | bytes 491528 | tf_op jit(solution)/shard_map/ppermute | solution.py:44
  162.0 13.6 %collective-permute-start.20 = (bf16[2,16,2560]{2,1,0:T(8,128)(2,1)S(1)}, bf16[2,16,2560]{2,1,0:T(8,128)(2,1)S(1)}, u32[]{:S(2)}, u32[]{:S(2)}) collective-permute-start(bf16[2,16,2560]{2,1,0:T(8,128)(2,1)S(1)} %get-tuple-element.56), channel_id=1, source_target_pairs={{0,16},{1,17},{16,0},{17,1},{2,18},{3,19},{18,2},{19,3},{4,20},{5,... | collective-permute-start | bytes 491528 | tf_op jit(solution)/shard_map/ppermute | solution.py:44
  163.5 12.0 %collective-permute-start.21 = (bf16[2,16,2560]{2,1,0:T(8,128)(2,1)S(1)}, bf16[2,16,2560]{2,1,0:T(8,128)(2,1)S(1)}, u32[]{:S(2)}, u32[]{:S(2)}) collective-permute-start(bf16[2,16,2560]{2,1,0:T(8,128)(2,1)S(1)} %get-tuple-element.55), channel_id=1, source_target_pairs={{0,17},{1,16},{16,1},{17,0},{2,19},{3,18},{18,3},{19,2},{4,21},{5,... | collective-permute-start | bytes 491528 | tf_op jit(solution)/shard_map/ppermute | solution.py:44
  165.2 10.0 %collective-permute-start.46 = (bf16[64,2560]{1,0:T(8,128)(2,1)S(1)}, bf16[64,2560]{1,0:T(8,128)(2,1)S(1)}, u32[]{:S(2)}, u32[]{:S(2)}) collective-permute-start(bf16[64,2560]{1,0:T(8,128)(2,1)S(1)} %fusion.26), channel_id=1, source_target_pairs={{0,2},{2,4},{4,6},{6,0},{1,3},{3,5},{5,7},{7,1},{8,10},{10,12},{12... | collective-permute-start | bytes 983048 | tf_op jit(solution)/shard_map/ppermute | solution.py:36
  (37 other events, 521.0 us)
where the time goes:
time: 186 us; the launch traced here: 185 us
  waiting for transfers between devices  81.4 us (44%)
  starting transfers between devices  48.6 us (26%)
  matrix products  31.6 us (17%)
  other arithmetic  11.9 us (6%)
  local copies, waits for them, and re-layouts  11 us (6%)
    ppermute x22, waiting for transfers between devices, rotated(): lax.ppermute(value, axis, [(i, (i + by) % size) for i in range(size)])  61.1 us
    ppermute x24, starting transfers between devices, in_plane(): return lax.ppermute(value, ('y', 'x'), route)  28.8 us
    ppermute x24, waiting for transfers between devices, in_plane(): return lax.ppermute(value, ('y', 'x'), route)  20.4 us
    dot_general x3, matrix products, expert_rows(): both = jnp.dot(rows_in, gate_up, preferred_element_type=jnp.float32)  14 us
    ppermute x22, starting transfers between devices, rotated(): lax.ppermute(value, axis, [(i, (i + by) % size) for i in range(size)])  12.9 us
    dot_general x3, matrix products, expert_rows(): jnp.dot(activated, down_rows, preferred_element_type=jnp.float32)  7.11 us
    ppermute x2, starting transfers between devices, shifted(): return lax.ppermute(block, axis, route)  6.9 us
    convert_element_type x3, other arithmetic, per_device(): running = total.astype(bf16)  4.25 us
  transfers between devices with their start and end apart: 48, of which 20 were waited for; matrix products, arithmetic and copies ran while one was open for 23% of the time, Pallas kernels for 0%

commit v1 on v0

--- a/solution.py
+++ b/solution.py
@@ -1,8 +1,11 @@
+import functools
 import math
 
 import jax
 import jax.numpy as jnp
 from jax import lax
+from jax.experimental import pallas as pl
+from jax.experimental.pallas import tpu as pltpu
 from jax.sharding import Mesh
 from jax.sharding import PartitionSpec as P
 
@@ -44,52 +47,78 @@
     return lax.ppermute(value, ("y", "x"), route)
 
 
-def window_attention(
-    query_rows, key_block, value_block, prior_keys, prior_values, sink_row, first_index, window_size
+def attention_kernel(
+    window, start_ref, sink_ref, query_ref, key_ref, value_ref, prior_ref, out_ref, keys, values
 ):
-    row_count = query_rows.shape[0]
-    head_width_dim = key_block.shape[1]
-    head_count = query_rows.shape[1] // head_width_dim
-    block_count = row_count // window_size
-    key_ext = jnp.concatenate([prior_keys, key_block], axis=0)
-    value_ext = jnp.concatenate([prior_values, value_block], axis=0)
-    key_block_tiles = jnp.concatenate(
-        [
-            key_ext[:row_count].reshape(block_count, window_size, head_width_dim),
-            key_block.reshape(block_count, window_size, head_width_dim),
+    block = pl.program_id(0)
+    width = key_ref.shape[0]
+    lanes = keys.shape[1]
+    share = lanes // width
+    heads = query_ref.shape[1] // width
+
+    @pl.when(block == 0)
+    def _():
+        scale = 1.0 / math.sqrt(width)
+        for half in range(share):
+            keys[half] = jnp.zeros(keys.shape[1:], keys.dtype)
+            values[half] = jnp.zeros(values.shape[1:], values.dtype)
+            at = slice(half * width, (half + 1) * width)
+            keys[half, at, :window] = (prior_ref[:width, :] * scale).astype(keys.dtype)
+            keys[half, at, window:] = (key_ref[...] * scale).astype(keys.dtype)
+            values[half, at, :window] = prior_ref[width:, :]
+            values[half, at, window:] = value_ref[...]
+
+    query_pos = lax.broadcasted_iota(jnp.int32, (window, 2 * window), 0)
+    key_pos = lax.broadcasted_iota(jnp.int32, (window, 2 * window), 1)
+    first = jnp.where((start_ref[0] == 0) & (block == 0), window, 0)
+    allowed = (key_pos > query_pos) & (key_pos <= query_pos + window) & (key_pos >= first)
+    span = pl.ds(pl.multiple_of(block * window, window), 2 * window)
+    for group in range(heads // share):
+        at = slice(group * lanes, (group + 1) * lanes)
+        query = query_ref[:, at]
+        mixed = jnp.zeros((window, lanes), jnp.float32)
+        for half in range(share):
+            scores = jnp.dot(query, keys[half, :, span], preferred_element_type=jnp.float32)
+            scores = jnp.where(allowed, scores, -jnp.inf)
+            sink = sink_ref[group * share + half]
+            highest = jnp.maximum(jnp.max(scores, axis=1, keepdims=True), sink)
+            raised = jnp.exp(scores - highest)
+            total = jnp.sum(raised, axis=1, keepdims=True) + jnp.exp(sink - highest)
+            probs = (raised * (1.0 / total)).astype(jnp.bfloat16)
+            mixed = mixed + lax.dot_general(
+                probs, values[half, :, span], (((1,), (1,)), ((), ())),
+                preferred_element_type=jnp.float32,
+            )
+        out_ref[:, at] = mixed.astype(out_ref.dtype)
+
+
+def window_attention(queries, keys_t, values_t, prior, sinks, start, window):
+    rows, columns = queries.shape
+    width = keys_t.shape[0]
+    lanes = 2 * width
+
+    def whole(array):
+        return pl.BlockSpec(array.shape, lambda i: (0, 0))
+
+    return pl.pallas_call(
+        functools.partial(attention_kernel, window),
+        out_shape=jax.ShapeDtypeStruct(queries.shape, queries.dtype),
+        grid=(rows // window,),
+        in_specs=[
+            pl.BlockSpec(memory_space=pltpu.SMEM),
+            pl.BlockSpec(memory_space=pltpu.SMEM),
+            pl.BlockSpec((window, columns), lambda i: (i, 0)),
+            whole(keys_t),
+            whole(values_t),
+            whole(prior),
         ],
-        axis=1,
-    )
-    value_block_tiles = jnp.concatenate(
-        [
-            value_ext[:row_count].reshape(block_count, window_size, head_width_dim),
-            value_block.reshape(block_count, window_size, head_width_dim),
+        out_specs=pl.BlockSpec((window, columns), lambda i: (i, 0)),
+        scratch_shapes=[
+            pltpu.VMEM((lanes // width, lanes, rows + window), keys_t.dtype),
+            pltpu.VMEM((lanes // width, lanes, rows + window), values_t.dtype),
         ],
-        axis=1,
-    )
-    query_block_tiles = query_rows.reshape(block_count, window_size, head_count, head_width_dim)
-    attention_scores = jnp.einsum(
-        "xnem,xcm->xenc", query_block_tiles, key_block_tiles, preferred_element_type=jnp.float32
-    ) * (1.0 / math.sqrt(head_width_dim))
-    query_pos = jnp.arange(window_size, dtype=jnp.int32)[:, None]
-    key_pos = jnp.arange(2 * window_size, dtype=jnp.int32)[None, :]
-    inside = (key_pos > query_pos) & (key_pos <= query_pos + window_size)
-    block_start = first_index + jnp.arange(block_count, dtype=jnp.int32) * window_size
-    present = block_start[:, None] - window_size + key_pos >= 0
-    allowed = inside[None, None, :, :] & present[:, None, None, :]
-    attention_scores = jnp.where(allowed, attention_scores, -jnp.inf)
-    sink_grid = sink_row[None, :, None, None]
-    highest = jnp.maximum(jnp.max(attention_scores, axis=-1, keepdims=True), sink_grid)
-    raised = jnp.exp(attention_scores - highest)
-    totals = jnp.sum(raised, axis=-1, keepdims=True) + jnp.exp(sink_grid - highest)
-    attention_probabilities = (raised / totals).astype(jnp.bfloat16)
-    mixed_value_rows = jnp.einsum(
-        "emjt,eta->ejma",
-        attention_probabilities,
-        value_block_tiles,
-        preferred_element_type=jnp.float32,
-    )
-    return mixed_value_rows.astype(jnp.bfloat16).reshape(row_count, head_count * head_width_dim)
+        name="window_attention",
+    )(start, sinks, queries, keys_t, values_t, prior)
 
 
 def expert_rows(rows_in, gate_up, down_rows):
@@ -144,9 +173,9 @@
             jnp.concatenate([other_values, value_piece], axis=1),
             jnp.concatenate([value_piece, other_values], axis=1),
         )
-    prior_keys, prior_values = shifted(
-        (key_piece[local_rows - WINDOW :], value_piece[local_rows - WINDOW :]), SEQ, 1
-    )
+    tail = slice(local_rows - WINDOW, local_rows)
+    keys_t, values_t = key_piece.T, value_piece.T
+    prior = shifted(jnp.concatenate([keys_t[:, tail], values_t[:, tail]], axis=0), SEQ, 1)
 
     flat_ids = expert_ids.reshape(-1)
     chosen = (flat_ids[:, None] == jnp.arange(expert_total, dtype=jnp.int32)[None, :]).astype(
@@ -164,15 +193,9 @@
     plane_slots = (((to_y * nc + to_c) * nz + zi) * nx + to_x) * cap + rank
     plane_rows = ny * nx * nc * cap
 
+    start = (seq_index * local_rows).reshape(1)
     attended = window_attention(
-        queries,
-        key_piece,
-        value_piece,
-        prior_keys,
-        prior_values,
-        sink_logits,
-        seq_index * local_rows,
-        WINDOW,
+        queries, keys_t, values_t, prior, sink_logits, start, WINDOW
     )
     partial = jnp.dot(attended, out_proj, preferred_element_type=f32).astype(bf16)
 

time: 186 us -> 188 us (1.011)
  waiting for transfers between devices: 81.4 us -> 91.2 us
  Pallas kernels: 0 us -> 6.27 us
  local copies, waits for them, and re-layouts: 11 us -> 6.42 us
  other arithmetic: 11.9 us -> 8.29 us
  starting transfers between devices: 48.6 us -> 45.5 us
  matrix products: 31.6 us -> 29.3 us
    ppermute x22, waiting for transfers between devices: 61.1 us -> 70.1 us  [rotated(): lax.ppermute(value, axis, [(i, (i + by) % size) for i in range(size)])]
    pallas_call x0 -> x1, Pallas kernels: none -> 6.27 us  [window_attention(): pl.pallas_call(functools.partial(attention_kernel, window), out_shape=jax...]
    ppermute x2 -> x1, starting transfers between devices: 6.9 us -> 2.39 us  [shifted(): return lax.ppermute(block, axis, route)]
    reshape x3 -> x0, local copies, waits for them, and re-layouts: 4.11 us -> none  [the longest x1 2.41 us: window_attention(): query_rows.reshape(block_count, window_size, head_count, head_width_dim)]
    dot_general x2 -> x0, matrix products: 3.31 us -> none  [the longest x1 2.11 us: window_attention(): jnp.einsum('xnem,xcm->xenc', query_block_tiles, key_block_tiles, preferre...]
  transfers between devices with their start and end apart: 48 -> 47, of which waited for: 20 -> 22; matrix products, arithmetic and copies ran while one was open for 23% -> 17% of each run, Pallas kernels for 0% -> 0%
where the time goes in v1:
time: 188 us
  waiting for transfers between devices  91.2 us (49%)
  starting transfers between devices  45.5 us (24%)
  matrix products  29.3 us (16%)
  other arithmetic  8.29 us (4%)
  local copies, waits for them, and re-layouts  6.42 us (3%)
  Pallas kernels  6.27 us (3%)
    ppermute x22, waiting for transfers between devices, rotated(): lax.ppermute(value, axis, [(i, (i + by) % size) for i in range(size)])  70.1 us
    ppermute x24, starting transfers between devices, in_plane(): return lax.ppermute(value, ('y', 'x'), route)  28.4 us
    ppermute x24, waiting for transfers between devices, in_plane(): return lax.ppermute(value, ('y', 'x'), route)  21.1 us
    ppermute x22, starting transfers between devices, rotated(): lax.ppermute(value, axis, [(i, (i + by) % size) for i in range(size)])  14.7 us
    dot_general x3, matrix products, expert_rows(): both = jnp.dot(rows_in, gate_up, preferred_element_type=jnp.float32)  14 us
    dot_general x3, matrix products, expert_rows(): jnp.dot(activated, down_rows, preferred_element_type=jnp.float32)  7.12 us
    pallas_call x1, Pallas kernels, window_attention(): pl.pallas_call(functools.partial(attention_kernel, window), out_shape=jax...  6.27 us
    convert_element_type x3, other arithmetic, per_device(): running = total.astype(bf16)  4.25 us
  transfers between devices with their start and end apart: 47, of which 22 were waited for; matrix products, arithmetic and copies ran while one was open for 17% of the time, Pallas kernels for 0%

profile of v1, /device:TPU:0, one launch (start us, length us, event | category | flops | bytes accessed | tf_op | source)
XLA Modules:
  0.0 187.8 jit_solution(2195435907204296684)
XLA Ops:
  1.6 2.4 %collective-permute-start = (bf16[128,128]{1,0:T(8,128)(2,1)S(1)}, bf16[128,128]{1,0:T(8,128)(2,1)S(1)}, u32[]{:S(2)}, u32[]{:S(2)}) collective-permute-start(bf16[128,128]{1,0:T(8,128)(2,1)S(1)} %pad_maximum_fusion.16), channel_id=1, source_target_pairs={{0,8},{8,16},{16,24},{1,9},{9,17},{17,25},{2,10},{10,18},{18,26},{... | collective-permute-start | bytes 98312 | tf_op jit(solution)/shard_map/ppermute | solution.py:34
  5.6 6.3 %window_attention.1 = bf16[512,512]{1,0:T(8,128)(2,1)} custom-call(s32[1]{0:T(128)} %bitcast.start_ref, f32[8]{0:T(128)} %sink_ref.1, bf16[512,512]{1,0:T(8,128)(2,1)} %query_ref.1, bf16[64,512]{1,0:T(8,128)(2,1)} %bitcast.266, bf16[64,512]{1,0:T(8,128)(2,1)} %bitcast.268, bf16[128,128]{1,0:T(8,128)(2,1)} %copy-done.3), custom_call_target="tpu_custom_call" | custom-call | tf_op jit(solution)/shard_map/window_attention/pallas_call | solution.py:103
  11.9 4.1 %convolution_convert_fusion = bf16[512,2560]{1,0:T(8,128)(2,1)} fusion(bf16[512,512]{1,0:T(8,128)(2,1)} %window_attention.1, bf16[512,2560]{1,0:T(8,128)(2,1)S(1)} %copy-done), kind=kOutput, calls=%fused_computation.12 | convolution fusion | flops 1343488000 | bytes 5767168 | tf_op jit(solution)/shard_map/dot_general | solution.py:200
  18.2 2.3 %collective-permute-start.4 = (bf16[64,2560]{1,0:T(8,128)(2,1)}, bf16[64,2560]{1,0:T(8,128)(2,1)}, u32[]{:S(2)}, u32[]{:S(2)}) collective-permute-start(bf16[64,2560]{1,0:T(8,128)(2,1)} %get-tuple-element.18), channel_id=1, source_target_pairs={{0,1},{1,0},{2,3},{3,2},{4,5},{5,4},{6,7},{7,6},{8,9},{9,8},{10,11... | collective-permute-start | bytes 983048 | tf_op jit(solution)/shard_map/ppermute | solution.py:39
  21.8 6.3 %collective-permute-done.4 = bf16[64,2560]{1,0:T(8,128)(2,1)} collective-permute-done((bf16[64,2560]{1,0:T(8,128)(2,1)}, bf16[64,2560]{1,0:T(8,128)(2,1)}, u32[]{:S(2)}, u32[]{:S(2)}) %collective-permute-start.4) | collective-permute-done | bytes 327712 | tf_op jit(solution)/shard_map/ppermute | solution.py:39
  29.9 2.6 %collective-permute-start.5 = (bf16[64,2560]{1,0:T(8,128)(2,1)}, bf16[64,2560]{1,0:T(8,128)(2,1)}, u32[]{:S(2)}, u32[]{:S(2)}) collective-permute-start(bf16[64,2560]{1,0:T(8,128)(2,1)} %add_convert_fusion.2), channel_id=1, source_target_pairs={{0,2},{2,4},{4,6},{6,0},{1,3},{3,5},{5,7},{7,1},{8,10},{10,12},{12... | collective-permute-start | bytes 983048 | tf_op jit(solution)/shard_map/ppermute | solution.py:39
  32.5 2.6 %collective-permute-start.32 = (f32[64,8]{0,1:T(8,128)S(1)}, f32[64,8]{0,1:T(8,128)S(1)}, u32[]{:S(2)}, u32[]{:S(2)}) collective-permute-start(f32[64,8]{0,1:T(8,128)S(1)} %pad_maximum_fusion.17), channel_id=1, source_target_pairs={{0,4},{2,6},{4,0},{6,2},{1,5},{3,7},{5,1},{7,3},{8,12},{10,14},{12... | collective-permute-start | bytes 6152 | tf_op jit(solution)/shard_map/ppermute | solution.py:39
  38.8 3.6 %collective-permute-done.5 = bf16[64,2560]{1,0:T(8,128)(2,1)} collective-permute-done((bf16[64,2560]{1,0:T(8,128)(2,1)}, bf16[64,2560]{1,0:T(8,128)(2,1)}, u32[]{:S(2)}, u32[]{:S(2)}) %collective-permute-start.5) | collective-permute-done | bytes 327712 | tf_op jit(solution)/shard_map/ppermute | solution.py:39
  47.7 8.5 %collective-permute-done.6 = bf16[64,2560]{1,0:T(8,128)(2,1)S(1)} collective-permute-done((bf16[64,2560]{1,0:T(8,128)(2,1)S(1)}, bf16[64,2560]{1,0:T(8,128)(2,1)S(1)}, u32[]{:S(2)}, u32[]{:S(2)}) %collective-permute-start.6) | collective-permute-done | bytes 327712 | tf_op jit(solution)/shard_map/ppermute | solution.py:39
  57.6 11.3 %collective-permute-done.7 = bf16[64,2560]{1,0:T(8,128)(2,1)S(1)} collective-permute-done((bf16[64,2560]{1,0:T(8,128)(2,1)S(1)}, bf16[64,2560]{1,0:T(8,128)(2,1)S(1)}, u32[]{:S(2)}, u32[]{:S(2)}) %collective-permute-start.7) | collective-permute-done | bytes 327712 | tf_op jit(solution)/shard_map/ppermute | solution.py:39
  74.7 4.1 %collective-permute-done.10 = bf16[2,16,2560]{2,1,0:T(8,128)(2,1)S(1)} collective-permute-done((bf16[2,16,2560]{2,1,0:T(8,128)(2,1)S(1)}, bf16[2,16,2560]{2,1,0:T(8,128)(2,1)S(1)}, u32[]{:S(2)}, u32[]{:S(2)}) %collective-permute-start.10) | collective-permute-done | bytes 163872 | tf_op jit(solution)/shard_map/ppermute | solution.py:47
  80.6 3.9 %collective-permute-done.12 = bf16[64,2560]{1,0:T(8,128)(2,1)S(1)} collective-permute-done((bf16[64,2560]{1,0:T(8,128)(2,1)S(1)}, bf16[64,2560]{1,0:T(8,128)(2,1)S(1)}, u32[]{:S(2)}, u32[]{:S(2)}) %collective-permute-start.12) | collective-permute-done | bytes 327712 | tf_op jit(solution)/shard_map/ppermute | solution.py:39
  90.7 2.7 %collective-permute-done.14 = bf16[2,16,2560]{2,1,0:T(8,128)(2,1)S(1)} collective-permute-done((bf16[2,16,2560]{2,1,0:T(8,128)(2,1)S(1)}, bf16[2,16,2560]{2,1,0:T(8,128)(2,1)S(1)}, u32[]{:S(2)}, u32[]{:S(2)}) %collective-permute-start.14) | collective-permute-done | bytes 163872 | tf_op jit(solution)/shard_map/ppermute | solution.py:47
  93.7 3.8 %collective-permute-done.22 = bf16[64,2560]{1,0:T(8,128)(2,1)S(1)} collective-permute-done((bf16[64,2560]{1,0:T(8,128)(2,1)S(1)}, bf16[64,2560]{1,0:T(8,128)(2,1)S(1)}, u32[]{:S(2)}, u32[]{:S(2)}) %collective-permute-start.22) | collective-permute-done | bytes 327712 | tf_op jit(solution)/shard_map/ppermute | solution.py:39
  103.3 3.1 %collective-permute-done.34 = bf16[2,16,2560]{2,1,0:T(8,128)(2,1)S(1)} collective-permute-done((bf16[2,16,2560]{2,1,0:T(8,128)(2,1)S(1)}, bf16[2,16,2560]{2,1,0:T(8,128)(2,1)S(1)}, u32[]{:S(2)}, u32[]{:S(2)}) %collective-permute-start.34) | collective-permute-done | bytes 163872 | tf_op jit(solution)/shard_map/ppermute | solution.py:47
  106.6 4.0 %collective-permute-done.23 = bf16[64,2560]{1,0:T(8,128)(2,1)S(1)} collective-permute-done((bf16[64,2560]{1,0:T(8,128)(2,1)S(1)}, bf16[64,2560]{1,0:T(8,128)(2,1)S(1)}, u32[]{:S(2)}, u32[]{:S(2)}) %collective-permute-start.23) | collective-permute-done | bytes 327712 | tf_op jit(solution)/shard_map/ppermute | solution.py:39
  114.8 5.6 %fusion.4 = f32[256,2880]{0,1:T(8,128)} fusion(bf16[256,2560]{1,0:T(8,128)(2,1)S(1)} %bitcast.216, bf16[1,2560,2880]{1,2,0:T(8,128)(2,1)S(1)} %bitcast.201), kind=kOutput, calls=%fused_computation.4 | convolution fusion | flops 3774873600 | bytes 19005440 | tf_op jit(solution)/shard_map/dot_general | solution.py:126
  120.4 4.2 %fusion.12 = bf16[256,2560]{1,0:T(8,128)(2,1)S(1)} fusion(bf16[1,1440,2560]{2,1,0:T(8,128)(2,1)S(1)} %bitcast.270, f32[256,2880]{0,1:T(8,128)} %fusion.4), kind=kOutput, calls=%fused_computation.13 | convolution fusion | flops 1891041280 | bytes 11632640 | tf_op jit(solution)/shard_map/dot_general | solution.py:132
  124.9 4.1 %fusion = f32[128,2880]{0,1:T(8,128)S(1)} fusion(bf16[128,2560]{1,0:T(8,128)(2,1)S(1)} %bitcast.210, bf16[1,2560,2880]{1,2,0:T(8,128)(2,1)S(1)} %bitcast.201), kind=kOutput, calls=%fused_computation | convolution fusion | flops 1887436800 | bytes 16875520 | tf_op jit(solution)/shard_map/dot_general | solution.py:126
  136.0 4.3 %fusion.2 = f32[128,2880]{0,1:T(8,128)S(1)} fusion(bf16[128,2560]{1,0:T(8,128)(2,1)S(1)} %bitcast.211, bf16[1,2560,2880]{1,2,0:T(8,128)(2,1)S(1)} %bitcast.201), kind=kOutput, calls=%fused_computation.2 | convolution fusion | flops 1887436800 | bytes 16875520 | tf_op jit(solution)/shard_map/dot_general | solution.py:126
  152.3 2.7 %collective-permute-done.42 = bf16[2,16,2560]{2,1,0:T(8,128)(2,1)S(1)} collective-permute-done((bf16[2,16,2560]{2,1,0:T(8,128)(2,1)S(1)}, bf16[2,16,2560]{2,1,0:T(8,128)(2,1)S(1)}, u32[]{:S(2)}, u32[]{:S(2)}) %collective-permute-start.42) | collective-permute-done | bytes 163872 | tf_op jit(solution)/shard_map/ppermute | solution.py:47
  156.9 7.6 %collective-permute-done.44 = bf16[64,2560]{1,0:T(8,128)(2,1)S(1)} collective-permute-done((bf16[64,2560]{1,0:T(8,128)(2,1)S(1)}, bf16[64,2560]{1,0:T(8,128)(2,1)S(1)}, u32[]{:S(2)}, u32[]{:S(2)}) %collective-permute-start.44) | collective-permute-done | bytes 327712 | tf_op jit(solution)/shard_map/ppermute | solution.py:39
  167.8 9.8 %collective-permute-done.45 = bf16[64,2560]{1,0:T(8,128)(2,1)S(1)} collective-permute-done((bf16[64,2560]{1,0:T(8,128)(2,1)S(1)}, bf16[64,2560]{1,0:T(8,128)(2,1)S(1)}, u32[]{:S(2)}, u32[]{:S(2)}) %collective-permute-start.45) | collective-permute-done | bytes 327712 | tf_op jit(solution)/shard_map/ppermute | solution.py:39
  178.3 8.5 %collective-permute-done.46 = bf16[64,2560]{1,0:T(8,128)(2,1)S(1)} collective-permute-done((bf16[64,2560]{1,0:T(8,128)(2,1)S(1)}, bf16[64,2560]{1,0:T(8,128)(2,1)S(1)}, u32[]{:S(2)}, u32[]{:S(2)}) %collective-permute-start.46) | collective-permute-done | bytes 327712 | tf_op jit(solution)/shard_map/ppermute | solution.py:39
  (177 shorter events, 68.7 us)
Async XLA Ops:
  18.2 9.9 %collective-permute-start.4 = (bf16[64,2560]{1,0:T(8,128)(2,1)}, bf16[64,2560]{1,0:T(8,128)(2,1)}, u32[]{:S(2)}, u32[]{:S(2)}) collective-permute-start(bf16[64,2560]{1,0:T(8,128)(2,1)} %get-tuple-element.18), channel_id=1, source_target_pairs={{0,1},{1,0},{2,3},{3,2},{4,5},{5,4},{6,7},{7,6},{8,9},{9,8},{10,11... | collective-permute-start | bytes 983048 | tf_op jit(solution)/shard_map/ppermute | solution.py:39
  21.7 15.5 %collective-permute-start.3 = (bf16[64,2560]{1,0:T(8,128)(2,1)S(1)}, bf16[64,2560]{1,0:T(8,128)(2,1)}, u32[]{:S(2)}, u32[]{:S(2)}) collective-permute-start(bf16[64,2560]{1,0:T(8,128)(2,1)S(1)} %get-tuple-element.19), channel_id=1, source_target_pairs={{0,1},{1,0},{2,3},{3,2},{4,5},{5,4},{6,7},{7,6},{8,9},{9,8},{10,11... | collective-permute-start | bytes 983048 | tf_op jit(solution)/shard_map/ppermute | solution.py:39
  29.9 12.5 %collective-permute-start.5 = (bf16[64,2560]{1,0:T(8,128)(2,1)}, bf16[64,2560]{1,0:T(8,128)(2,1)}, u32[]{:S(2)}, u32[]{:S(2)}) collective-permute-start(bf16[64,2560]{1,0:T(8,128)(2,1)} %add_convert_fusion.2), channel_id=1, source_target_pairs={{0,2},{2,4},{4,6},{6,0},{1,3},{3,5},{5,7},{7,1},{8,10},{10,12},{12... | collective-permute-start | bytes 983048 | tf_op jit(solution)/shard_map/ppermute | solution.py:39
  32.5 11.4 %collective-permute-start.32 = (f32[64,8]{0,1:T(8,128)S(1)}, f32[64,8]{0,1:T(8,128)S(1)}, u32[]{:S(2)}, u32[]{:S(2)}) collective-permute-start(f32[64,8]{0,1:T(8,128)S(1)} %pad_maximum_fusion.17), channel_id=1, source_target_pairs={{0,4},{2,6},{4,0},{6,2},{1,5},{3,7},{5,1},{7,3},{8,12},{10,14},{12... | collective-permute-start | bytes 6152 | tf_op jit(solution)/shard_map/ppermute | solution.py:39
  36.5 20.8 %collective-permute-start.11 = (f32[64,8]{0,1:T(8,128)S(1)}, f32[64,8]{0,1:T(8,128)S(1)}, u32[]{:S(2)}, u32[]{:S(2)}) collective-permute-start(f32[64,8]{0,1:T(8,128)S(1)} %pad_maximum_fusion.17), channel_id=1, source_target_pairs={{0,2},{2,4},{4,6},{6,0},{1,3},{3,5},{5,7},{7,1},{8,10},{10,12},{12... | collective-permute-start | bytes 6152 | tf_op jit(solution)/shard_map/ppermute | solution.py:39
  37.2 10.5 %collective-permute-start.2 = (bf16[64,2560]{1,0:T(8,128)(2,1)S(1)}, bf16[64,2560]{1,0:T(8,128)(2,1)S(1)}, u32[]{:S(2)}, u32[]{:S(2)}) collective-permute-start(bf16[64,2560]{1,0:T(8,128)(2,1)S(1)} %get-tuple-element.20), channel_id=1, source_target_pairs={{0,1},{1,0},{2,3},{3,2},{4,5},{5,4},{6,7},{7,6},{8,9},{9,8},{10,11... | collective-permute-start | bytes 983048 | tf_op jit(solution)/shard_map/ppermute | solution.py:39
  43.7 12.4 %collective-permute-start.6 = (bf16[64,2560]{1,0:T(8,128)(2,1)S(1)}, bf16[64,2560]{1,0:T(8,128)(2,1)S(1)}, u32[]{:S(2)}, u32[]{:S(2)}) collective-permute-start(bf16[64,2560]{1,0:T(8,128)(2,1)S(1)} %add_convert_fusion.1), channel_id=1, source_target_pairs={{0,2},{2,4},{4,6},{6,0},{1,3},{3,5},{5,7},{7,1},{8,10},{10,12},{12... | collective-permute-start | bytes 983048 | tf_op jit(solution)/shard_map/ppermute | solution.py:39
  44.0 13.6 %collective-permute-start.1 = (bf16[64,2560]{1,0:T(8,128)(2,1)S(1)}, bf16[64,2560]{1,0:T(8,128)(2,1)S(1)}, u32[]{:S(2)}, u32[]{:S(2)}) collective-permute-start(bf16[64,2560]{1,0:T(8,128)(2,1)S(1)} %get-tuple-element.17), channel_id=1, source_target_pairs={{0,1},{1,0},{2,3},{3,2},{4,5},{5,4},{6,7},{7,6},{8,9},{9,8},{10,11... | collective-permute-start | bytes 983048 | tf_op jit(solution)/shard_map/ppermute | solution.py:39
  57.3 11.6 %collective-permute-start.7 = (bf16[64,2560]{1,0:T(8,128)(2,1)S(1)}, bf16[64,2560]{1,0:T(8,128)(2,1)S(1)}, u32[]{:S(2)}, u32[]{:S(2)}) collective-permute-start(bf16[64,2560]{1,0:T(8,128)(2,1)S(1)} %add_convert_fusion), channel_id=1, source_target_pairs={{0,2},{2,4},{4,6},{6,0},{1,3},{3,5},{5,7},{7,1},{8,10},{10,12},{12... | collective-permute-start | bytes 983048 | tf_op jit(solution)/shard_map/ppermute | solution.py:39
  74.6 9.9 %collective-permute-start.12 = (bf16[64,2560]{1,0:T(8,128)(2,1)S(1)}, bf16[64,2560]{1,0:T(8,128)(2,1)S(1)}, u32[]{:S(2)}, u32[]{:S(2)}) collective-permute-start(bf16[64,2560]{1,0:T(8,128)(2,1)S(1)} %multiply_convert_fusion), channel_id=1, source_target_pairs={{0,2},{2,4},{4,6},{6,0},{1,3},{3,5},{5,7},{7,1},{8,10},{10,12},{12... | collective-permute-start | bytes 983048 | tf_op jit(solution)/shard_map/ppermute | solution.py:39
  93.6 21.0 %collective-permute-start.16 = (bf16[2,4,16,2560]{3,2,1,0:T(8,128)(2,1)S(1)}, bf16[2,4,16,2560]{3,2,1,0:T(8,128)(2,1)S(1)}, u32[]{:S(2)}, u32[]{:S(2)}) collective-permute-start(bf16[2,4,16,2560]{3,2,1,0:T(8,128)(2,1)S(1)} %pad_maximum_fusion.3), channel_id=1, source_target_pairs={{0,8},{8,0},{1,9},{9,1},{2,10},{10,2},{3,11},{11,3},{4,12},{12,4},... | collective-permute-start | bytes 1966088 | tf_op jit(solution)/shard_map/ppermute | solution.py:39
  106.5 18.3 %collective-permute-start.36 = (bf16[1,4,16,2560]{3,2,1,0:T(8,128)(2,1)S(1)}, bf16[1,4,16,2560]{3,2,1,0:T(8,128)(2,1)S(1)}, u32[]{:S(2)}, u32[]{:S(2)}) collective-permute-start(bf16[1,4,16,2560]{3,2,1,0:T(8,128)(2,1)S(1)} %get-tuple-element.36), channel_id=1, source_target_pairs={{0,8},{8,0},{1,9},{9,1},{2,10},{10,2},{3,11},{11,3},{4,12},{12,4},... | collective-permute-start | bytes 983048 | tf_op jit(solution)/shard_map/ppermute | solution.py:39
  111.1 20.0 %collective-permute-start.24 = (bf16[2,16,2560]{2,1,0:T(8,128)(2,1)S(1)}, bf16[2,16,2560]{2,1,0:T(8,128)(2,1)S(1)}, u32[]{:S(2)}, u32[]{:S(2)}) collective-permute-start(bf16[2,16,2560]{2,1,0:T(8,128)(2,1)S(1)} %bitcast.238), channel_id=1, source_target_pairs={{0,1},{1,0},{16,17},{17,16},{2,3},{3,2},{18,19},{19,18},{4,5},{5,4... | collective-permute-start | bytes 491528 | tf_op jit(solution)/shard_map/ppermute | solution.py:47
  112.5 18.6 %collective-permute-start.25 = (bf16[2,16,2560]{2,1,0:T(8,128)(2,1)S(1)}, bf16[2,16,2560]{2,1,0:T(8,128)(2,1)S(1)}, u32[]{:S(2)}, u32[]{:S(2)}) collective-permute-start(bf16[2,16,2560]{2,1,0:T(8,128)(2,1)S(1)} %bitcast.236), channel_id=1, source_target_pairs={{0,16},{1,17},{16,0},{17,1},{2,18},{3,19},{18,2},{19,3},{4,20},{5,... | collective-permute-start | bytes 491528 | tf_op jit(solution)/shard_map/ppermute | solution.py:47
  112.7 18.3 %collective-permute-start.26 = (bf16[2,16,2560]{2,1,0:T(8,128)(2,1)S(1)}, bf16[2,16,2560]{2,1,0:T(8,128)(2,1)S(1)}, u32[]{:S(2)}, u32[]{:S(2)}) collective-permute-start(bf16[2,16,2560]{2,1,0:T(8,128)(2,1)S(1)} %bitcast.233), channel_id=1, source_target_pairs={{0,17},{1,16},{16,1},{17,0},{2,19},{3,18},{18,3},{19,2},{4,21},{5,... | collective-permute-start | bytes 491528 | tf_op jit(solution)/shard_map/ppermute | solution.py:47
  124.7 19.1 %collective-permute-start.17 = (bf16[2,4,16,2560]{3,2,1,0:T(8,128)(2,1)S(1)}, bf16[2,4,16,2560]{3,2,1,0:T(8,128)(2,1)S(1)}, u32[]{:S(2)}, u32[]{:S(2)}) collective-permute-start(bf16[2,4,16,2560]{3,2,1,0:T(8,128)(2,1)S(1)} %bitcast.222), channel_id=1, source_target_pairs={{0,8},{8,0},{1,9},{9,1},{2,10},{10,2},{3,11},{11,3},{4,12},{12,4},... | collective-permute-start | bytes 1966088 | tf_op jit(solution)/shard_map/ppermute | solution.py:39
  144.7 10.3 %collective-permute-start.42 = (bf16[2,16,2560]{2,1,0:T(8,128)(2,1)S(1)}, bf16[2,16,2560]{2,1,0:T(8,128)(2,1)S(1)}, u32[]{:S(2)}, u32[]{:S(2)}) collective-permute-start(bf16[2,16,2560]{2,1,0:T(8,128)(2,1)S(1)} %get-tuple-element.26), channel_id=1, source_target_pairs={{0,16},{1,17},{16,0},{17,1},{2,18},{3,19},{18,2},{19,3},{4,20},{5,... | collective-permute-start | bytes 491528 | tf_op jit(solution)/shard_map/ppermute | solution.py:47
  147.6 18.1 %collective-permute-start.29 = (bf16[2,16,2560]{2,1,0:T(8,128)(2,1)S(1)}, bf16[2,16,2560]{2,1,0:T(8,128)(2,1)S(1)}, u32[]{:S(2)}, u32[]{:S(2)}) collective-permute-start(bf16[2,16,2560]{2,1,0:T(8,128)(2,1)S(1)} %get-tuple-element.42), channel_id=1, source_target_pairs={{0,1},{1,0},{16,17},{17,16},{2,3},{3,2},{18,19},{19,18},{4,5},{5,4... | collective-permute-start | bytes 491528 | tf_op jit(solution)/shard_map/ppermute | solution.py:47
  148.3 19.1 %collective-permute-start.30 = (bf16[2,16,2560]{2,1,0:T(8,128)(2,1)S(1)}, bf16[2,16,2560]{2,1,0:T(8,128)(2,1)S(1)}, u32[]{:S(2)}, u32[]{:S(2)}) collective-permute-start(bf16[2,16,2560]{2,1,0:T(8,128)(2,1)S(1)} %get-tuple-element.44), channel_id=1, source_target_pairs={{0,16},{1,17},{16,0},{17,1},{2,18},{3,19},{18,2},{19,3},{4,20},{5,... | collective-permute-start | bytes 491528 | tf_op jit(solution)/shard_map/ppermute | solution.py:47
  150.9 16.5 %collective-permute-start.31 = (bf16[2,16,2560]{2,1,0:T(8,128)(2,1)S(1)}, bf16[2,16,2560]{2,1,0:T(8,128)(2,1)S(1)}, u32[]{:S(2)}, u32[]{:S(2)}) collective-permute-start(bf16[2,16,2560]{2,1,0:T(8,128)(2,1)S(1)} %get-tuple-element.43), channel_id=1, source_target_pairs={{0,17},{1,16},{16,1},{17,0},{2,19},{3,18},{18,3},{19,2},{4,21},{5,... | collective-permute-start | bytes 491528 | tf_op jit(solution)/shard_map/ppermute | solution.py:47
  155.7 22.2 %collective-permute-start.18 = (bf16[2,16,2560]{2,1,0:T(8,128)(2,1)S(1)}, bf16[2,16,2560]{2,1,0:T(8,128)(2,1)S(1)}, u32[]{:S(2)}, u32[]{:S(2)}) collective-permute-start(bf16[2,16,2560]{2,1,0:T(8,128)(2,1)S(1)} %get-tuple-element.54), channel_id=1, source_target_pairs={{0,1},{1,0},{16,17},{17,16},{2,3},{3,2},{18,19},{19,18},{4,5},{5,4... | collective-permute-start | bytes 491528 | tf_op jit(solution)/shard_map/ppermute | solution.py:47
  164.5 13.4 %collective-permute-start.19 = (bf16[2,16,2560]{2,1,0:T(8,128)(2,1)S(1)}, bf16[2,16,2560]{2,1,0:T(8,128)(2,1)S(1)}, u32[]{:S(2)}, u32[]{:S(2)}) collective-permute-start(bf16[2,16,2560]{2,1,0:T(8,128)(2,1)S(1)} %get-tuple-element.56), channel_id=1, source_target_pairs={{0,16},{1,17},{16,0},{17,1},{2,18},{3,19},{18,2},{19,3},{4,20},{5,... | collective-permute-start | bytes 491528 | tf_op jit(solution)/shard_map/ppermute | solution.py:47
  165.6 12.3 %collective-permute-start.20 = (bf16[2,16,2560]{2,1,0:T(8,128)(2,1)S(1)}, bf16[2,16,2560]{2,1,0:T(8,128)(2,1)S(1)}, u32[]{:S(2)}, u32[]{:S(2)}) collective-permute-start(bf16[2,16,2560]{2,1,0:T(8,128)(2,1)S(1)} %get-tuple-element.55), channel_id=1, source_target_pairs={{0,17},{1,16},{16,1},{17,0},{2,19},{3,18},{18,3},{19,2},{4,21},{5,... | collective-permute-start | bytes 491528 | tf_op jit(solution)/shard_map/ppermute | solution.py:47
  167.4 10.2 %collective-permute-start.45 = (bf16[64,2560]{1,0:T(8,128)(2,1)S(1)}, bf16[64,2560]{1,0:T(8,128)(2,1)S(1)}, u32[]{:S(2)}, u32[]{:S(2)}) collective-permute-start(bf16[64,2560]{1,0:T(8,128)(2,1)S(1)} %fusion.25), channel_id=1, source_target_pairs={{0,2},{2,4},{4,6},{6,0},{1,3},{3,5},{5,7},{7,1},{8,10},{10,12},{12... | collective-permute-start | bytes 983048 | tf_op jit(solution)/shard_map/ppermute | solution.py:39
  (36 other events, 530.8 us)
